TPU v7x, 128 devices: a whole 4x4x4 slice. The times are simulated.
128 devices in a mesh: ctx: 64 (over y_hi, z, x, core), head: 2 (over y_lo).
Axes of the slice: x: 4, y: 4 (y_hi: 2, y_lo: 2; y = y_hi * 2 + y_lo), z: 4, core: 2. Of those that a mesh axis runs over, the one named last changes fastest.
Arguments:
- queries: bfloat16 [16384, 8192], P('ctx', 'head'), may hold values from -5 to 5
- keys: bfloat16 [16384, 512], P(('ctx', 'head')), may hold values from -5 to 5
- values: bfloat16 [16384, 512], P(('ctx', 'head')), may hold values from -6 to 6
- d_out: bfloat16 [16384, 8192], P('ctx', 'head'), may hold values from -6 to 6
- selected: int32 [256, 12], P('ctx'), may hold values from 0 to 11, as said below
- partners: int32 [2, 64], replicated, may hold values from 0 to 63, as said below
Outputs:
- attended: bfloat16 [16384, 8192], P('ctx', 'head')
- grad_queries: bfloat16 [16384, 8192], P('ctx', 'head')
- grad_keys: bfloat16 [16384, 512], P(('ctx', 'head'))
- grad_values: bfloat16 [16384, 512], P(('ctx', 'head'))
Inputs may be any that keep to these rules, and one draw needn't show every extreme that they name: `selected`: row b lists 12 different candidate blocks of query block b: 0 to 3 are its own shard's key blocks, 4 to 7 those of its partner under the first matching, 8 to 11 those under the second; the first entry is the query block's own key block (b modulo 4). `partners`: row r gives for every shard i its partner i XOR m_r, with a mask m_r that is the same for all shards; one of the two masks is 32, the other is 2 ** j - 1 for some j of 1 to 6, and either may stand in either row.
All inputs are finite; a program needn't handle non-finite values.
Results may differ from a plain program's by a relative error of at most 0.018.
Values may be sent and summed in bfloat16 or wider, within the bound.
No kernel may reach another device: no remote copies, remote signals or barrier semaphores. Data moves between devices by JAX's collectives and lax.ppermute only.
A program may use at most 128 MiB of HBM per device.

v0:
```python
import jax
import jax.numpy as jnp
from jax import lax
from jax.sharding import PartitionSpec as P

HQ = 64
KVH = 4
DH = 128
BLK = 64
SEL = 12


def from_partner(value, axis, distance):
    mask = 2**distance
    pairs = [(source, source ^ mask) for source in range(lax.axis_size(axis))]
    return lax.ppermute(value, axis, pairs)


def keep_or_take(current, arrived, mask_value, bit_number):
    bit_set = mask_value // 2**bit_number % 2 == 1
    return tuple(
        (jnp.where(bit_set, new_part, old_part) for old_part, new_part in zip(current, arrived))
    )


def return_pairs(pair_first, pair_second, mask_first, mask_second, bit_total):
    for bit_number in range(bit_total):
        swapped = from_partner(
            (pair_first[0], pair_first[1], pair_second[0], pair_second[1]), "ctx", bit_number
        )
        pair_first = keep_or_take(pair_first, swapped[0:2], mask_first, bit_number)
        pair_second = keep_or_take(pair_second, swapped[2:4], mask_second, bit_number)
    return (pair_first, pair_second)


def body(queries, keys, values, d_out, selected, partners):
    head_count = lax.axis_size("head")
    kv_local = KVH // head_count
    group_size = HQ // KVH
    tokens_dev = queries.shape[0]
    query_width = queries.shape[1]
    block_count = tokens_dev // BLK
    cand_blocks = 3 * block_count
    kv_width = kv_local * DH
    score_scale = DH ** (-0.5)
    keys_local, values_local = (
        lax.all_to_all(keys, "head", split_axis=1, concat_axis=0, tiled=True),
        lax.all_to_all(values, "head", split_axis=1, concat_axis=0, tiled=True),
    )
    mask_first = partners[0, 0]
    mask_second = partners[1, 0]
    bit_total = lax.axis_size("ctx").bit_length() - 1
    every_key, every_value = (
        lax.all_gather(keys_local, "ctx", axis=0, tiled=True),
        lax.all_gather(values_local, "ctx", axis=0, tiled=True),
    )
    own_index = lax.axis_index("ctx")

    def shard_rows(source, mask_value):
        row_start = jnp.bitwise_xor(own_index, mask_value) * tokens_dev
        return lax.dynamic_slice_in_dim(source, row_start, tokens_dev, 0)

    pair_first = (shard_rows(every_key, mask_first), shard_rows(every_value, mask_first))
    pair_second = (shard_rows(every_key, mask_second), shard_rows(every_value, mask_second))
    cand_keys = jnp.concatenate([keys_local, pair_first[0], pair_second[0]], 0).reshape(
        cand_blocks, BLK, kv_local, DH
    )
    cand_values = jnp.concatenate([values_local, pair_first[1], pair_second[1]], 0).reshape(
        cand_blocks, BLK, kv_local, DH
    )
    cand_ids = jnp.arange(cand_blocks, dtype=jnp.int32)

    def one_block(block_index, loop_state):
        out_all, grad_q_all, key_terms, value_terms = loop_state
        row_start = block_index * BLK
        query_block = lax.dynamic_slice_in_dim(queries, row_start, BLK, 0).reshape(
            BLK, kv_local, group_size, DH
        )
        grad_block = lax.dynamic_slice_in_dim(d_out, row_start, BLK, 0).reshape(
            BLK, kv_local, group_size, DH
        )
        chosen = lax.dynamic_index_in_dim(selected, block_index, 0, keepdims=False)
        picked_keys = jnp.take(cand_keys, chosen, axis=0).reshape(SEL * BLK, kv_local, DH)
        picked_values = jnp.take(cand_values, chosen, axis=0).reshape(SEL * BLK, kv_local, DH)
        scores = (
            jnp.einsum(
                "qgrd,kgd->grqk", query_block, picked_keys, preferred_element_type=jnp.float32
            )
            * score_scale
        )
        row_max = jnp.max(scores, axis=-1, keepdims=True)
        exp_scores = jnp.exp(scores - row_max)
        prob_full = exp_scores / jnp.sum(exp_scores, axis=-1, keepdims=True)
        prob_low = prob_full.astype(jnp.bfloat16)
        out_block = jnp.einsum(
            "grqk,kgd->qgrd", prob_low, picked_values, preferred_element_type=jnp.float32
        ).astype(jnp.bfloat16)
        grad_p = jnp.einsum(
            "qgrd,kgd->grqk", grad_block, picked_values, preferred_element_type=jnp.float32
        )
        row_delta = jnp.einsum(
            "qgrd,qgrd->grq", grad_block, out_block, preferred_element_type=jnp.float32
        )
        grad_s = (prob_full * (grad_p - row_delta[..., None]) * score_scale).astype(jnp.bfloat16)
        grad_q = jnp.einsum(
            "grqk,kgd->qgrd", grad_s, picked_keys, preferred_element_type=jnp.float32
        ).astype(jnp.bfloat16)
        key_part = jnp.einsum(
            "grqk,qgrd->kgd", grad_s, query_block, preferred_element_type=jnp.float32
        ).reshape(SEL, BLK * kv_width)
        value_part = jnp.einsum(
            "grqk,qgrd->kgd", prob_low, grad_block, preferred_element_type=jnp.float32
        ).reshape(SEL, BLK * kv_width)
        one_hot = (chosen[:, None] == cand_ids[None, :]).astype(jnp.float32)
        key_terms = key_terms + jnp.dot(
            one_hot.T, key_part, precision=lax.Precision.HIGHEST, preferred_element_type=jnp.float32
        )
        value_terms = value_terms + jnp.dot(
            one_hot.T,
            value_part,
            precision=lax.Precision.HIGHEST,
            preferred_element_type=jnp.float32,
        )
        out_all = lax.dynamic_update_slice_in_dim(
            out_all, out_block.reshape(BLK, query_width), row_start, 0
        )
        grad_q_all = lax.dynamic_update_slice_in_dim(
            grad_q_all, grad_q.reshape(BLK, query_width), row_start, 0
        )
        return (out_all, grad_q_all, key_terms, value_terms)

    start_state = (
        jnp.zeros((tokens_dev, query_width), jnp.bfloat16),
        jnp.zeros((tokens_dev, query_width), jnp.bfloat16),
        jnp.zeros((cand_blocks, BLK * kv_width), jnp.float32),
        jnp.zeros((cand_blocks, BLK * kv_width), jnp.float32),
    )
    attended, grad_queries, key_terms, value_terms = lax.fori_loop(
        0, block_count, one_block, start_state
    )
    first_terms = (
        key_terms[block_count : 2 * block_count].astype(jnp.bfloat16),
        value_terms[block_count : 2 * block_count].astype(jnp.bfloat16),
    )
    second_terms = (
        key_terms[2 * block_count :].astype(jnp.bfloat16),
        value_terms[2 * block_count :].astype(jnp.bfloat16),
    )
    back_first, back_second = return_pairs(
        first_terms, second_terms, mask_first, mask_second, bit_total
    )
    key_total = (
        key_terms[:block_count]
        + back_first[0].astype(jnp.float32)
        + back_second[0].astype(jnp.float32)
    )
    value_total = (
        value_terms[:block_count]
        + back_first[1].astype(jnp.float32)
        + back_second[1].astype(jnp.float32)
    )
    key_rows = key_total.reshape(tokens_dev, kv_width).astype(jnp.bfloat16)
    value_rows = value_total.reshape(tokens_dev, kv_width).astype(jnp.bfloat16)
    grad_keys, grad_values = (
        lax.all_to_all(key_rows, "head", split_axis=0, concat_axis=1, tiled=True),
        lax.all_to_all(value_rows, "head", split_axis=0, concat_axis=1, tiled=True),
    )
    return (attended, grad_queries, grad_keys, grad_values)


def solution(mesh):
    return jax.shard_map(
        body,
        mesh=mesh,
        in_specs=(
            P("ctx", "head"),
            P(("ctx", "head"), None),
            P(("ctx", "head"), None),
            P("ctx", "head"),
            P("ctx", None),
            P(),
        ),
        out_specs=(
            P("ctx", "head"),
            P("ctx", "head"),
            P(("ctx", "head"), None),
            P(("ctx", "head"), None),
        ),
        check_vma=False,
    )
```

profile of v0, /device:TPU:0, one launch (start us, length us, event | category | flops | bytes accessed | tf_op | source)
XLA Modules:
  0.0 422.1 jit_solution(7663354984939706454)
XLA Ops:
  8.4 7.5 %all_to_all.70 = bf16[128,2,256]{2,0,1:T(8,128)(2,1)} all-to-all(bf16[128,2,256]{2,0,1:T(8,128)(2,1)S(1)} %copy.61), channel_id=1, replica_groups=mesh['ctx'=64,'head'=2] {'head'}, dimensions={1} | all-to-all | bytes 262144 | tf_op jit(solution)/shard_map/all_to_all | solution.py:47
  17.1 7.5 %all_to_all.71 = bf16[128,2,256]{2,0,1:T(8,128)(2,1)} all-to-all(bf16[128,2,256]{2,0,1:T(8,128)(2,1)S(1)} %copy.59), channel_id=1, replica_groups=mesh['ctx'=64,'head'=2] {'head'}, dimensions={1} | all-to-all | bytes 262144 | tf_op jit(solution)/shard_map/all_to_all | solution.py:48
  32.9 66.7 %all-gather.5.cloned.1.call-done = bf16[16384,256]{1,0:T(8,128)(2,1)} async-done(((bf16[256,256]{1,0:T(8,128)(2,1)}), bf16[16384,256]{1,0:T(8,128)(2,1)}) %all-gather.5.cloned.1.call-update) | async-done | bytes 8388624 | tf_op jit(solution)/shard_map/all_gather | solution.py:54
  99.6 81.9 %all-gather.3.cloned.1.call-done = bf16[16384,256]{1,0:T(8,128)(2,1)} async-done(((bf16[256,256]{1,0:T(8,128)(2,1)}), bf16[16384,256]{1,0:T(8,128)(2,1)}) %all-gather.3.cloned.1.call-update) | async-done | bytes 8388624 | tf_op jit(solution)/shard_map/all_gather | solution.py:55
  187.7 157.0 %while.20 = (s32[]{:T(128)}, bf16[256,4096]{1,0:T(8,128)(2,1)}, bf16[256,4096]{1,0:T(8,128)(2,1)}, f32[12,16384]{1,0:T(8,128)}, f32[12,16384]{1,0:T(8,128)}, /*i...) while((s32[]{:T(128)}, bf16[256,4096]{1,0:T(8,128)(2,1)}, ...), condition=%wide.region_3.5_spmd.clone, body=%wide.region_0.4_spmd.clone.sunk | while | flops 2491023616 | bytes 80786256 | solution.py:138
  195.4 4.7 %fusion.96 = (f32[2,16,64]{2,1,0:T(8,128)S(1)}, f32[2,16,64,768]{3,2,1,0:T(8,128)}) fusion(bf16[64,2,16,128]{3,2,1,0:T(8,128)(2,1)S(1)} %bitcast.140, bf16[768,2,128,1]{2,1,0,3:T(2,128)(2,1)S(1)} %bitcast.138), kind=kOutput, calls=%fused_computation.82.clone.1 | convolution fusion | flops 407372544 | bytes 7217152 | tf_op jit(solution)/shard_map/while/body/eval_jaxpr/sub | solution.py:92
  200.1 3.2 fusion.97
  205.5 3.1 fusion.101
  210.1 3.6 fusion.98
  232.8 4.7 %fusion.96 = (f32[2,16,64]{2,1,0:T(8,128)S(1)}, f32[2,16,64,768]{3,2,1,0:T(8,128)}) fusion(bf16[64,2,16,128]{3,2,1,0:T(8,128)(2,1)S(1)} %bitcast.140, bf16[768,2,128,1]{2,1,0,3:T(2,128)(2,1)S(1)} %bitcast.138), kind=kOutput, calls=%fused_computation.82.clone.1 | convolution fusion | flops 407372544 | bytes 7217152 | tf_op jit(solution)/shard_map/while/body/eval_jaxpr/sub | solution.py:92
  237.5 3.2 fusion.97
  242.9 3.1 fusion.101
  247.5 3.6 fusion.98
  257.0 2.9 convolution_add_fusion.4
  260.6 3.0 convolution_add_fusion.5
  272.6 4.7 %fusion.96 = (f32[2,16,64]{2,1,0:T(8,128)S(1)}, f32[2,16,64,768]{3,2,1,0:T(8,128)}) fusion(bf16[64,2,16,128]{3,2,1,0:T(8,128)(2,1)S(1)} %bitcast.140, bf16[768,2,128,1]{2,1,0,3:T(2,128)(2,1)S(1)} %bitcast.138), kind=kOutput, calls=%fused_computation.82.clone.1 | convolution fusion | flops 407372544 | bytes 7217152 | tf_op jit(solution)/shard_map/while/body/eval_jaxpr/sub | solution.py:92
  277.3 3.2 fusion.97
  282.8 3.1 fusion.101
  287.3 3.6 fusion.98
  296.9 2.9 convolution_add_fusion.4
  300.5 3.0 convolution_add_fusion.5
  312.5 4.7 %fusion.96 = (f32[2,16,64]{2,1,0:T(8,128)S(1)}, f32[2,16,64,768]{3,2,1,0:T(8,128)}) fusion(bf16[64,2,16,128]{3,2,1,0:T(8,128)(2,1)S(1)} %bitcast.140, bf16[768,2,128,1]{2,1,0,3:T(2,128)(2,1)S(1)} %bitcast.138), kind=kOutput, calls=%fused_computation.82.clone.1 | convolution fusion | flops 407372544 | bytes 7217152 | tf_op jit(solution)/shard_map/while/body/eval_jaxpr/sub | solution.py:92
  317.2 3.2 fusion.97
  322.7 3.1 fusion.101
  327.2 3.6 fusion.98
  336.8 2.9 convolution_add_fusion.4
  340.3 3.0 convolution_add_fusion.5
  355.3 3.1 collective-permute-start.14
  361.3 2.7 collective-permute-start.2
  398.7 3.4 all-to-all-start.3
  406.5 3.4 all-to-all-start.2
  410.8 3.6 all-to-all-done.2
  (231 shorter events, 144.0 us)
Async XLA Ops:
  7.2 92.4 %all-gather.5.cloned.1.call-start = ((), (), s32[]{:S(2)}) async-start(), calls=%async_computation.5 | async-start | bytes 8519680 | tf_op jit(solution)/shard_map/all_gather | solution.py:54
  15.9 165.5 %all-gather.3.cloned.1.call-start = ((), (), s32[]{:S(2)}) async-start(), calls=%async_computation.4 | async-start | bytes 8519680 | tf_op jit(solution)/shard_map/all_gather | solution.py:55
  24.6 159.8 %copy-start.6 = (bf16[128,2,256]{2,0,1:T(8,128)(2,1)S(1)}, bf16[128,2,256]{2,0,1:T(8,128)(2,1)}, u32[]{:S(2)}) copy-start(bf16[128,2,256]{2,0,1:T(8,128)(2,1)} %all_to_all.71) | copy-start | bytes 393220
  225.0 7.4 %copy-start.2 = (bf16[12,64,2,128]{3,2,1,0:T(2,128)(2,1)}, bf16[12,64,2,128]{3,2,1,0:T(2,128)(2,1)S(1)}, u32[]{:S(2)}) copy-start(bf16[12,64,2,128]{3,2,1,0:T(2,128)(2,1)S(1)} %get-tuple-element.396) | copy-start | bytes 1179652 | tf_op jit(solution)/shard_map/while
  264.9 7.4 %copy-start.2 = (bf16[12,64,2,128]{3,2,1,0:T(2,128)(2,1)}, bf16[12,64,2,128]{3,2,1,0:T(2,128)(2,1)S(1)}, u32[]{:S(2)}) copy-start(bf16[12,64,2,128]{3,2,1,0:T(2,128)(2,1)S(1)} %get-tuple-element.396) | copy-start | bytes 1179652 | tf_op jit(solution)/shard_map/while
  304.8 7.4 %copy-start.2 = (bf16[12,64,2,128]{3,2,1,0:T(2,128)(2,1)}, bf16[12,64,2,128]{3,2,1,0:T(2,128)(2,1)S(1)}, u32[]{:S(2)}) copy-start(bf16[12,64,2,128]{3,2,1,0:T(2,128)(2,1)S(1)} %get-tuple-element.396) | copy-start | bytes 1179652 | tf_op jit(solution)/shard_map/while
  346.1 2.6 collective-permute-start.12
  346.4 2.3 collective-permute-start.18
  348.1 2.9 collective-permute-start
  348.4 2.6 collective-permute-start.6
  348.8 6.4 %collective-permute-start.13 = (bf16[4,16384]{1,0:T(4,128)(2,1)S(1)}, bf16[4,16384]{1,0:T(4,128)(2,1)S(1)}, u32[]{:S(2)}, u32[]{:S(2)}) collective-permute-start(bf16[4,16384]{1,0:T(4,128)(2,1)S(1)} %get-tuple-element.269), channel_id=1, source_target_pairs={{0,4},{2,6},{4,0},{6,2},{8,12},{10,14},{12,8},{14,10},{16,20},{18,... | collective-permute-start | bytes 393224 | tf_op jit(solution)/shard_map/ppermute | solution.py:16
  350.4 8.0 %collective-permute-start.19 = (bf16[4,16384]{1,0:T(4,128)(2,1)S(1)}, bf16[4,16384]{1,0:T(4,128)(2,1)S(1)}, u32[]{:S(2)}, u32[]{:S(2)}) collective-permute-start(bf16[4,16384]{1,0:T(4,128)(2,1)S(1)} %get-tuple-element.270), channel_id=1, source_target_pairs={{0,4},{2,6},{4,0},{6,2},{8,12},{10,14},{12,8},{14,10},{16,20},{18,... | collective-permute-start | bytes 393224 | tf_op jit(solution)/shard_map/ppermute | solution.py:16
  351.1 10.1 %collective-permute-start.1 = (bf16[4,16384]{1,0:T(4,128)(2,1)S(1)}, bf16[4,16384]{1,0:T(4,128)(2,1)S(1)}, u32[]{:S(2)}, u32[]{:S(2)}) collective-permute-start(bf16[4,16384]{1,0:T(4,128)(2,1)S(1)} %get-tuple-element.273), channel_id=1, source_target_pairs={{0,4},{2,6},{4,0},{6,2},{8,12},{10,14},{12,8},{14,10},{16,20},{18,... | collective-permute-start | bytes 393224 | tf_op jit(solution)/shard_map/ppermute | solution.py:16
  352.7 11.3 %collective-permute-start.7 = (bf16[4,16384]{1,0:T(4,128)(2,1)S(1)}, bf16[4,16384]{1,0:T(4,128)(2,1)S(1)}, u32[]{:S(2)}, u32[]{:S(2)}) collective-permute-start(bf16[4,16384]{1,0:T(4,128)(2,1)S(1)} %get-tuple-element.274), channel_id=1, source_target_pairs={{0,4},{2,6},{4,0},{6,2},{8,12},{10,14},{12,8},{14,10},{16,20},{18,... | collective-permute-start | bytes 393224 | tf_op jit(solution)/shard_map/ppermute | solution.py:16
  355.3 13.3 %collective-permute-start.14 = (bf16[4,16384]{1,0:T(4,128)(2,1)S(1)}, bf16[4,16384]{1,0:T(4,128)(2,1)S(1)}, u32[]{:S(2)}, u32[]{:S(2)}) collective-permute-start(bf16[4,16384]{1,0:T(4,128)(2,1)S(1)} %broadcast_select_fusion.14), channel_id=1, source_target_pairs={{0,8},{2,10},{4,12},{6,14},{8,0},{10,2},{12,4},{14,6},{16,24},{18,... | collective-permute-start | bytes 393224 | tf_op jit(solution)/shard_map/ppermute | solution.py:16
  358.5 13.0 %collective-permute-start.20 = (bf16[4,16384]{1,0:T(4,128)(2,1)S(1)}, bf16[4,16384]{1,0:T(4,128)(2,1)S(1)}, u32[]{:S(2)}, u32[]{:S(2)}) collective-permute-start(bf16[4,16384]{1,0:T(4,128)(2,1)S(1)} %broadcast_select_fusion.4), channel_id=1, source_target_pairs={{0,8},{2,10},{4,12},{6,14},{8,0},{10,2},{12,4},{14,6},{16,24},{18,... | collective-permute-start | bytes 393224 | tf_op jit(solution)/shard_map/ppermute | solution.py:16
  361.3 13.0 %collective-permute-start.2 = (bf16[4,16384]{1,0:T(4,128)(2,1)S(1)}, bf16[4,16384]{1,0:T(4,128)(2,1)S(1)}, u32[]{:S(2)}, u32[]{:S(2)}) collective-permute-start(bf16[4,16384]{1,0:T(4,128)(2,1)S(1)} %broadcast_select_fusion.15), channel_id=1, source_target_pairs={{0,8},{2,10},{4,12},{6,14},{8,0},{10,2},{12,4},{14,6},{16,24},{18,... | collective-permute-start | bytes 393224 | tf_op jit(solution)/shard_map/ppermute | solution.py:16
  364.1 12.3 %collective-permute-start.8 = (bf16[4,16384]{1,0:T(4,128)(2,1)S(1)}, bf16[4,16384]{1,0:T(4,128)(2,1)S(1)}, u32[]{:S(2)}, u32[]{:S(2)}) collective-permute-start(bf16[4,16384]{1,0:T(4,128)(2,1)S(1)} %broadcast_select_fusion.5), channel_id=1, source_target_pairs={{0,8},{2,10},{4,12},{6,14},{8,0},{10,2},{12,4},{14,6},{16,24},{18,... | collective-permute-start | bytes 393224 | tf_op jit(solution)/shard_map/ppermute | solution.py:16
  368.7 7.9 %collective-permute-start.15 = (bf16[4,16384]{1,0:T(4,128)(2,1)S(1)}, bf16[4,16384]{1,0:T(4,128)(2,1)S(1)}, u32[]{:S(2)}, u32[]{:S(2)}) collective-permute-start(bf16[4,16384]{1,0:T(4,128)(2,1)S(1)} %broadcast_select_fusion.16), channel_id=1, source_target_pairs={{0,16},{2,18},{4,20},{6,22},{8,24},{10,26},{12,28},{14,30},{16,0},... | collective-permute-start | bytes 393224 | tf_op jit(solution)/shard_map/ppermute | solution.py:16
  371.5 7.4 %collective-permute-start.21 = (bf16[4,16384]{1,0:T(4,128)(2,1)S(1)}, bf16[4,16384]{1,0:T(4,128)(2,1)S(1)}, u32[]{:S(2)}, u32[]{:S(2)}) collective-permute-start(bf16[4,16384]{1,0:T(4,128)(2,1)S(1)} %broadcast_select_fusion.6), channel_id=1, source_target_pairs={{0,16},{2,18},{4,20},{6,22},{8,24},{10,26},{12,28},{14,30},{16,0},... | collective-permute-start | bytes 393224 | tf_op jit(solution)/shard_map/ppermute | solution.py:16
  374.3 6.2 %collective-permute-start.3 = (bf16[4,16384]{1,0:T(4,128)(2,1)S(1)}, bf16[4,16384]{1,0:T(4,128)(2,1)S(1)}, u32[]{:S(2)}, u32[]{:S(2)}) collective-permute-start(bf16[4,16384]{1,0:T(4,128)(2,1)S(1)} %broadcast_select_fusion.17), channel_id=1, source_target_pairs={{0,16},{2,18},{4,20},{6,22},{8,24},{10,26},{12,28},{14,30},{16,0},... | collective-permute-start | bytes 393224 | tf_op jit(solution)/shard_map/ppermute | solution.py:16
  376.4 6.6 %collective-permute-start.9 = (bf16[4,16384]{1,0:T(4,128)(2,1)S(1)}, bf16[4,16384]{1,0:T(4,128)(2,1)S(1)}, u32[]{:S(2)}, u32[]{:S(2)}) collective-permute-start(bf16[4,16384]{1,0:T(4,128)(2,1)S(1)} %broadcast_select_fusion.7), channel_id=1, source_target_pairs={{0,16},{2,18},{4,20},{6,22},{8,24},{10,26},{12,28},{14,30},{16,0},... | collective-permute-start | bytes 393224 | tf_op jit(solution)/shard_map/ppermute | solution.py:16
  376.7 9.4 %collective-permute-start.16 = (bf16[4,16384]{1,0:T(4,128)(2,1)S(1)}, bf16[4,16384]{1,0:T(4,128)(2,1)S(1)}, u32[]{:S(2)}, u32[]{:S(2)}) collective-permute-start(bf16[4,16384]{1,0:T(4,128)(2,1)S(1)} %broadcast_select_fusion.18), channel_id=1, source_target_pairs={{0,32},{2,34},{4,36},{6,38},{8,40},{10,42},{12,44},{14,46},{16,48}... | collective-permute-start | bytes 393224 | tf_op jit(solution)/shard_map/ppermute | solution.py:16
  379.0 9.9 %collective-permute-start.22 = (bf16[4,16384]{1,0:T(4,128)(2,1)S(1)}, bf16[4,16384]{1,0:T(4,128)(2,1)S(1)}, u32[]{:S(2)}, u32[]{:S(2)}) collective-permute-start(bf16[4,16384]{1,0:T(4,128)(2,1)S(1)} %broadcast_select_fusion.8), channel_id=1, source_target_pairs={{0,32},{2,34},{4,36},{6,38},{8,40},{10,42},{12,44},{14,46},{16,48}... | collective-permute-start | bytes 393224 | tf_op jit(solution)/shard_map/ppermute | solution.py:16
  380.6 11.2 %collective-permute-start.4 = (bf16[4,16384]{1,0:T(4,128)(2,1)S(1)}, bf16[4,16384]{1,0:T(4,128)(2,1)S(1)}, u32[]{:S(2)}, u32[]{:S(2)}) collective-permute-start(bf16[4,16384]{1,0:T(4,128)(2,1)S(1)} %broadcast_select_fusion.19), channel_id=1, source_target_pairs={{0,32},{2,34},{4,36},{6,38},{8,40},{10,42},{12,44},{14,46},{16,48}... | collective-permute-start | bytes 393224 | tf_op jit(solution)/shard_map/ppermute | solution.py:16
  383.1 10.5 %collective-permute-start.10 = (bf16[4,16384]{1,0:T(4,128)(2,1)S(1)}, bf16[4,16384]{1,0:T(4,128)(2,1)S(1)}, u32[]{:S(2)}, u32[]{:S(2)}) collective-permute-start(bf16[4,16384]{1,0:T(4,128)(2,1)S(1)} %broadcast_select_fusion.9), channel_id=1, source_target_pairs={{0,32},{2,34},{4,36},{6,38},{8,40},{10,42},{12,44},{14,46},{16,48}... | collective-permute-start | bytes 393224 | tf_op jit(solution)/shard_map/ppermute | solution.py:16
  386.2 9.4 %collective-permute-start.17 = (bf16[4,16384]{1,0:T(4,128)(2,1)S(1)}, bf16[4,16384]{1,0:T(4,128)(2,1)S(1)}, u32[]{:S(2)}, u32[]{:S(2)}) collective-permute-start(bf16[4,16384]{1,0:T(4,128)(2,1)S(1)} %broadcast_select_fusion.20), channel_id=1, source_target_pairs={{0,64},{2,66},{4,68},{6,70},{8,72},{10,74},{12,76},{14,78},{16,80}... | collective-permute-start | bytes 393224 | tf_op jit(solution)/shard_map/ppermute | solution.py:16
  389.0 7.8 %collective-permute-start.23 = (bf16[4,16384]{1,0:T(4,128)(2,1)S(1)}, bf16[4,16384]{1,0:T(4,128)(2,1)S(1)}, u32[]{:S(2)}, u32[]{:S(2)}) collective-permute-start(bf16[4,16384]{1,0:T(4,128)(2,1)S(1)} %broadcast_select_fusion.10), channel_id=1, source_target_pairs={{0,64},{2,66},{4,68},{6,70},{8,72},{10,74},{12,76},{14,78},{16,80}... | collective-permute-start | bytes 393224 | tf_op jit(solution)/shard_map/ppermute | solution.py:16
  391.8 10.3 %collective-permute-start.5 = (bf16[4,16384]{1,0:T(4,128)(2,1)S(1)}, bf16[4,16384]{1,0:T(4,128)(2,1)S(1)}, u32[]{:S(2)}, u32[]{:S(2)}) collective-permute-start(bf16[4,16384]{1,0:T(4,128)(2,1)S(1)} %broadcast_select_fusion.21), channel_id=1, source_target_pairs={{0,64},{2,66},{4,68},{6,70},{8,72},{10,74},{12,76},{14,78},{16,80}... | collective-permute-start | bytes 393224 | tf_op jit(solution)/shard_map/ppermute | solution.py:16
  393.7 8.4 %collective-permute-start.11 = (bf16[4,16384]{1,0:T(4,128)(2,1)S(1)}, bf16[4,16384]{1,0:T(4,128)(2,1)S(1)}, u32[]{:S(2)}, u32[]{:S(2)}) collective-permute-start(bf16[4,16384]{1,0:T(4,128)(2,1)S(1)} %broadcast_select_fusion.11), channel_id=1, source_target_pairs={{0,64},{2,66},{4,68},{6,70},{8,72},{10,74},{12,76},{14,78},{16,80}... | collective-permute-start | bytes 393224 | tf_op jit(solution)/shard_map/ppermute | solution.py:16
  398.7 7.8 %all-to-all-start.3 = ((bf16[2,128,256]{2,1,0:T(8,128)(2,1)}), bf16[2,128,256]{2,1,0:T(8,128)(2,1)S(1)}, u32[]{:S(2)}, u32[]{:S(2)}) async-start(bf16[2,128,256]{2,1,0:T(8,128)(2,1)} %convert_element_type.74), calls=%async_computation.3 | async-start | bytes 262144 | tf_op jit(solution)/shard_map/all_to_all | solution.py:166
  406.5 7.8 %all-to-all-start.2 = ((bf16[2,128,256]{2,1,0:T(8,128)(2,1)}), bf16[2,128,256]{2,1,0:T(8,128)(2,1)S(1)}, u32[]{:S(2)}, u32[]{:S(2)}) async-start(bf16[2,128,256]{2,1,0:T(8,128)(2,1)} %convert_element_type.70), calls=%async_computation.2 | async-start | bytes 262144 | tf_op jit(solution)/shard_map/all_to_all | solution.py:165
  (21 other events, 76.3 us)
Sparse Core Ops, SparseCore 0:
  16.0 83.4 all-gather.4
  102.7 78.6 all-gather.2
where the time goes:
time: 424 us; the launch traced here: 422 us
  waiting for transfers between devices  173 us (41%)
  matrix products  88.8 us (21%)
  local copies, waits for them, and re-layouts  60.4 us (14%)
  starting transfers between devices  36.1 us (9%)
  other arithmetic  26.8 us (6%)
  between operations  21.2 us (5%)
  blocking collectives  15 us (4%)
    all_gather x1, waiting for transfers between devices, body(): lax.all_gather(values_local, 'ctx', axis=0, tiled=True)  81.9 us
    all_gather x1, waiting for transfers between devices, body(): lax.all_gather(keys_local, 'ctx', axis=0, tiled=True)  66.7 us
    ppermute x24, starting transfers between devices, from_partner(): return lax.ppermute(value, axis, pairs)  29.3 us
    sub x4, matrix products, one_block(): exp_scores = jnp.exp(scores - row_max)  18.8 us
    ppermute x24, waiting for transfers between devices, from_partner(): return lax.ppermute(value, axis, pairs)  18.5 us
    dot_general x4, matrix products, one_block(): jnp.einsum('qgrd,kgd->grqk', grad_block, picked_values, preferred_element...  14.5 us
    convert_element_type x4, other arithmetic, one_block(): prob_low = prob_full.astype(jnp.bfloat16)  12.9 us
    dot_general x4, matrix products, one_block(): jnp.einsum('grqk,qgrd->kgd', prob_low, grad_block, preferred_element_type...  12.5 us
  transfers between devices with their start and end apart: 28, of which 15 were waited for; matrix products, arithmetic and copies ran while one was open for 2% of the time, Pallas kernels for 0%

commit v1 on v0

--- a/solution.py
+++ b/solution.py
@@ -52,7 +52,9 @@
     bit_total = lax.axis_size("ctx").bit_length() - 1
     every_key, every_value = (
         lax.all_gather(keys_local, "ctx", axis=0, tiled=True),
-        lax.all_gather(values_local, "ctx", axis=0, tiled=True),
+        jnp.concatenate(
+            lax.all_to_all(jnp.stack([values_local] * lax.axis_size("ctx")), "ctx", 0, 0), axis=0
+        ),
     )
     own_index = lax.axis_index("ctx")
 

time: 424 us -> 447 us (1.054)
  local copies, waits for them, and re-layouts: 60.4 us -> 92.7 us
  matrix products: 88.8 us -> 76.3 us
  starting transfers between devices: 36.1 us -> 48 us
  waiting for transfers between devices: 173 us -> 165 us
    all_to_all x0 -> x1, waiting for transfers between devices: none -> 99.2 us  [body(): lax.all_to_all(jnp.stack([values_local] * lax.axis_size('ctx')), 'ctx', 0...]
    all_gather x1 -> x0, waiting for transfers between devices: 81.9 us -> none  [body(): lax.all_gather(values_local, 'ctx', axis=0, tiled=True)]
    all_gather x1, waiting for transfers between devices: 66.7 us -> 41.6 us  [body(): lax.all_gather(keys_local, 'ctx', axis=0, tiled=True)]
    all_to_all x0 -> x1, starting transfers between devices: none -> 11.9 us  [body(): lax.all_to_all(jnp.stack([values_local] * lax.axis_size('ctx')), 'ctx', 0...]
    while x64 -> x104, local copies, waits for them, and re-layouts: 9.47 us -> 21.3 us
    reshape x4, local copies, waits for them, and re-layouts: 2.52 us -> 11 us  [one_block(): key_part = jnp.einsum('grqk,qgrd->kgd', grad_s, query_block, preferred_el...]
    dot_general x4, matrix products: 14.5 us -> 6.43 us  [one_block(): jnp.einsum('qgrd,kgd->grqk', grad_block, picked_values, preferred_element...]
    dot_general x4, matrix products: 10.7 us -> 3.49 us  [one_block(): jnp.dot(one_hot.T, value_part, precision=lax.Precision.HIGHEST, preferred...]
  transfers between devices with their start and end apart: 28 -> 28, of which waited for: 15 -> 15; matrix products, arithmetic and copies ran while one was open for 2% -> 3% of each run, Pallas kernels for 0% -> 0%
where the time goes in v1:
time: 447 us; the launch traced here: 445 us
  waiting for transfers between devices  165 us (37%)
  local copies, waits for them, and re-layouts  92.7 us (21%)
  matrix products  76.3 us (17%)
  starting transfers between devices  48 us (11%)
  other arithmetic  25.9 us (6%)
  between operations  21.1 us (5%)
  blocking collectives  14.4 us (3%)
    all_to_all x1, waiting for transfers between devices, body(): lax.all_to_all(jnp.stack([values_local] * lax.axis_size('ctx')), 'ctx', 0...  99.2 us
    all_gather x1, waiting for transfers between devices, body(): lax.all_gather(keys_local, 'ctx', axis=0, tiled=True)  41.6 us
    ppermute x24, starting transfers between devices, from_partner(): return lax.ppermute(value, axis, pairs)  29.3 us
    while x104, local copies, waits for them, and re-layouts  21.3 us
    sub x4, matrix products, one_block(): exp_scores = jnp.exp(scores - row_max)  18.8 us
    ppermute x24, waiting for transfers between devices, from_partner(): return lax.ppermute(value, axis, pairs)  18.5 us
    convert_element_type x4, other arithmetic, one_block(): prob_low = prob_full.astype(jnp.bfloat16)  12.9 us
    dot_general x4, matrix products, one_block(): jnp.dot(one_hot.T, key_part, precision=lax.Precision.HIGHEST, preferred_e...  12.8 us
  transfers between devices with their start and end apart: 28, of which 15 were waited for; matrix products, arithmetic and copies ran while one was open for 3% of the time, Pallas kernels for 0%

profile of v1, /device:TPU:0, one launch (start us, length us, event | category | flops | bytes accessed | tf_op | source)
XLA Modules:
  0.0 444.6 jit_solution(8164516251626761168)
XLA Ops:
  8.4 7.5 %all_to_all.75 = bf16[128,2,256]{2,0,1:T(8,128)(2,1)} all-to-all(bf16[128,2,256]{2,0,1:T(8,128)(2,1)S(1)} %copy.61), channel_id=1, replica_groups=mesh['ctx'=64,'head'=2] {'head'}, dimensions={1} | all-to-all | bytes 262144 | tf_op jit(solution)/shard_map/all_to_all | solution.py:47
  17.1 6.8 %all_to_all.76 = bf16[128,2,256]{2,0,1:T(8,128)(2,1)S(1)} all-to-all(bf16[128,2,256]{2,0,1:T(8,128)(2,1)S(1)} %copy.59), channel_id=1, replica_groups=mesh['ctx'=64,'head'=2] {'head'}, dimensions={1} | all-to-all | bytes 262144 | tf_op jit(solution)/shard_map/all_to_all | solution.py:48
  23.9 4.3 stack.2
  28.2 11.9 %all-to-all-start.1 = ((bf16[64,256,256]{2,1,0:T(8,128)(2,1)}), bf16[64,256,256]{2,1,0:T(8,128)(2,1)}, u32[]{:S(2)}, u32[]{:S(2)}) async-start(bf16[64,256,256]{2,1,0:T(8,128)(2,1)} %stack.2), calls=%async_computation.1 | async-start | bytes 16777216 | tf_op jit(solution)/shard_map/all_to_all | solution.py:56
  47.6 99.2 %all-to-all-done.1 = bf16[64,256,256]{2,1,0:T(8,128)(2,1)} async-done(((bf16[64,256,256]{2,1,0:T(8,128)(2,1)}), bf16[64,256,256]{2,1,0:T(8,128)(2,1)}, u32[]{:S(2)}, u32[]{:S(2)}) %all-to-all-start.1) | async-done | bytes 8388640 | tf_op jit(solution)/shard_map/all_to_all | solution.py:56
  146.8 41.6 %all-gather.2.cloned.1.call-done = bf16[16384,256]{1,0:T(8,128)(2,1)} async-done(((bf16[256,256]{1,0:T(8,128)(2,1)}), bf16[16384,256]{1,0:T(8,128)(2,1)}) %all-gather.2.cloned.1.call-update) | async-done | bytes 8388624 | tf_op jit(solution)/shard_map/all_gather | solution.py:54
  194.5 172.6 %while.20 = (s32[]{:T(128)}, bf16[256,4096]{1,0:T(8,128)(2,1)}, bf16[256,4096]{1,0:T(8,128)(2,1)}, f32[12,16384]{1,0:T(8,128)}, f32[12,16384]{1,0:T(8,128)}, /*i...) while((s32[]{:T(128)}, bf16[256,4096]{1,0:T(8,128)(2,1)}, ...), condition=%wide.region_3.5_spmd.clone, body=%wide.region_0.4_spmd.clone.sunk | while | flops 2491023616 | bytes 112244064 | solution.py:140
  202.5 4.7 %fusion.96 = (f32[2,16,64]{2,1,0:T(8,128)S(1)}, f32[2,16,64,768]{3,2,1,0:T(8,128)}) fusion(bf16[64,2,16,128]{3,2,1,0:T(8,128)(2,1)S(1)} %bitcast.141, bf16[768,2,128,1]{2,1,0,3:T(2,128)(2,1)S(1)} %bitcast.139), kind=kOutput, calls=%fused_computation.82.clone.1 | convolution fusion | flops 407372544 | bytes 7217152 | tf_op jit(solution)/shard_map/while/body/eval_jaxpr/sub | solution.py:94
  207.2 3.2 fusion.97
  219.3 3.1 fusion.100
  224.5 2.8 reshape.157
  227.3 3.0 convolution_add_fusion.4
  230.3 3.1 fusion.101
  245.4 4.7 %fusion.96 = (f32[2,16,64]{2,1,0:T(8,128)S(1)}, f32[2,16,64,768]{3,2,1,0:T(8,128)}) fusion(bf16[64,2,16,128]{3,2,1,0:T(8,128)(2,1)S(1)} %bitcast.141, bf16[768,2,128,1]{2,1,0,3:T(2,128)(2,1)S(1)} %bitcast.139), kind=kOutput, calls=%fused_computation.82.clone.1 | convolution fusion | flops 407372544 | bytes 7217152 | tf_op jit(solution)/shard_map/while/body/eval_jaxpr/sub | solution.py:94
  250.1 3.2 fusion.97
  262.2 3.1 fusion.100
  270.2 3.3 convolution_add_fusion.4
  273.5 3.1 fusion.101
  288.7 4.7 %fusion.96 = (f32[2,16,64]{2,1,0:T(8,128)S(1)}, f32[2,16,64,768]{3,2,1,0:T(8,128)}) fusion(bf16[64,2,16,128]{3,2,1,0:T(8,128)(2,1)S(1)} %bitcast.141, bf16[768,2,128,1]{2,1,0,3:T(2,128)(2,1)S(1)} %bitcast.139), kind=kOutput, calls=%fused_computation.82.clone.1 | convolution fusion | flops 407372544 | bytes 7217152 | tf_op jit(solution)/shard_map/while/body/eval_jaxpr/sub | solution.py:94
  293.4 3.2 fusion.97
  305.5 3.1 fusion.100
  313.5 3.3 convolution_add_fusion.4
  316.7 3.1 fusion.101
  331.9 4.7 %fusion.96 = (f32[2,16,64]{2,1,0:T(8,128)S(1)}, f32[2,16,64,768]{3,2,1,0:T(8,128)}) fusion(bf16[64,2,16,128]{3,2,1,0:T(8,128)(2,1)S(1)} %bitcast.141, bf16[768,2,128,1]{2,1,0,3:T(2,128)(2,1)S(1)} %bitcast.139), kind=kOutput, calls=%fused_computation.82.clone.1 | convolution fusion | flops 407372544 | bytes 7217152 | tf_op jit(solution)/shard_map/while/body/eval_jaxpr/sub | solution.py:94
  336.6 3.2 fusion.97
  348.7 3.1 fusion.100
  356.7 3.3 convolution_add_fusion.4
  360.0 3.1 fusion.101
  377.8 3.1 collective-permute-start.14
  421.2 3.4 all-to-all-start.4
  429.0 3.4 all-to-all-start.3
  433.3 3.6 all-to-all-done.3
  (273 shorter events, 165.4 us)
Async XLA Ops:
  7.2 181.2 %all-gather.2.cloned.1.call-start = ((), (), s32[]{:S(2)}) async-start(), calls=%async_computation.5 | async-start | bytes 8519680 | tf_op jit(solution)/shard_map/all_gather | solution.py:54
  28.2 11.9 %copy-start.12 = (s32[2,64]{1,0:T(2,128)S(1)}, s32[2,64]{1,0:T(2,128)}, u32[]{:S(2)}) copy-start(s32[2,64]{1,0:T(2,128)} %param.15) | copy-start | bytes 1540
  28.2 161.3 %copy-start.9 = (bf16[128,2,256]{2,0,1:T(8,128)(2,1)S(1)}, bf16[128,2,256]{2,0,1:T(8,128)(2,1)}, u32[]{:S(2)}) copy-start(bf16[128,2,256]{2,0,1:T(8,128)(2,1)} %all_to_all.75) | copy-start | bytes 393220
  28.2 118.6 %all-to-all-start.1 = ((bf16[64,256,256]{2,1,0:T(8,128)(2,1)}), bf16[64,256,256]{2,1,0:T(8,128)(2,1)}, u32[]{:S(2)}, u32[]{:S(2)}) async-start(bf16[64,256,256]{2,1,0:T(8,128)(2,1)} %stack.2), calls=%async_computation.1 | async-start | bytes 16777216 | tf_op jit(solution)/shard_map/all_to_all | solution.py:56
  262.2 8.0 %copy-start.11 = (s32[12]{0:T(128)S(1)}, s32[12]{0:T(128)}, u32[]{:S(2)}) copy-start(s32[12]{0:T(128)} %copy-done.10) | copy-start | bytes 148 | tf_op jit(solution)/shard_map/while
  305.5 8.0 %copy-start.11 = (s32[12]{0:T(128)S(1)}, s32[12]{0:T(128)}, u32[]{:S(2)}) copy-start(s32[12]{0:T(128)} %copy-done.10) | copy-start | bytes 148 | tf_op jit(solution)/shard_map/while
  368.5 2.6 collective-permute-start.12
  368.9 2.3 collective-permute-start.18
  370.5 2.9 collective-permute-start
  370.8 2.6 collective-permute-start.6
  371.3 6.4 %collective-permute-start.13 = (bf16[4,16384]{1,0:T(4,128)(2,1)S(1)}, bf16[4,16384]{1,0:T(4,128)(2,1)S(1)}, u32[]{:S(2)}, u32[]{:S(2)}) collective-permute-start(bf16[4,16384]{1,0:T(4,128)(2,1)S(1)} %get-tuple-element.269), channel_id=1, source_target_pairs={{0,4},{2,6},{4,0},{6,2},{8,12},{10,14},{12,8},{14,10},{16,20},{18,... | collective-permute-start | bytes 393224 | tf_op jit(solution)/shard_map/ppermute | solution.py:16
  372.8 8.0 %collective-permute-start.19 = (bf16[4,16384]{1,0:T(4,128)(2,1)S(1)}, bf16[4,16384]{1,0:T(4,128)(2,1)S(1)}, u32[]{:S(2)}, u32[]{:S(2)}) collective-permute-start(bf16[4,16384]{1,0:T(4,128)(2,1)S(1)} %get-tuple-element.270), channel_id=1, source_target_pairs={{0,4},{2,6},{4,0},{6,2},{8,12},{10,14},{12,8},{14,10},{16,20},{18,... | collective-permute-start | bytes 393224 | tf_op jit(solution)/shard_map/ppermute | solution.py:16
  373.6 10.1 %collective-permute-start.1 = (bf16[4,16384]{1,0:T(4,128)(2,1)S(1)}, bf16[4,16384]{1,0:T(4,128)(2,1)S(1)}, u32[]{:S(2)}, u32[]{:S(2)}) collective-permute-start(bf16[4,16384]{1,0:T(4,128)(2,1)S(1)} %get-tuple-element.273), channel_id=1, source_target_pairs={{0,4},{2,6},{4,0},{6,2},{8,12},{10,14},{12,8},{14,10},{16,20},{18,... | collective-permute-start | bytes 393224 | tf_op jit(solution)/shard_map/ppermute | solution.py:16
  375.1 11.3 %collective-permute-start.7 = (bf16[4,16384]{1,0:T(4,128)(2,1)S(1)}, bf16[4,16384]{1,0:T(4,128)(2,1)S(1)}, u32[]{:S(2)}, u32[]{:S(2)}) collective-permute-start(bf16[4,16384]{1,0:T(4,128)(2,1)S(1)} %get-tuple-element.274), channel_id=1, source_target_pairs={{0,4},{2,6},{4,0},{6,2},{8,12},{10,14},{12,8},{14,10},{16,20},{18,... | collective-permute-start | bytes 393224 | tf_op jit(solution)/shard_map/ppermute | solution.py:16
  377.8 13.3 %collective-permute-start.14 = (bf16[4,16384]{1,0:T(4,128)(2,1)S(1)}, bf16[4,16384]{1,0:T(4,128)(2,1)S(1)}, u32[]{:S(2)}, u32[]{:S(2)}) collective-permute-start(bf16[4,16384]{1,0:T(4,128)(2,1)S(1)} %broadcast_select_fusion.14), channel_id=1, source_target_pairs={{0,8},{2,10},{4,12},{6,14},{8,0},{10,2},{12,4},{14,6},{16,24},{18,... | collective-permute-start | bytes 393224 | tf_op jit(solution)/shard_map/ppermute | solution.py:16
  380.9 13.0 %collective-permute-start.20 = (bf16[4,16384]{1,0:T(4,128)(2,1)S(1)}, bf16[4,16384]{1,0:T(4,128)(2,1)S(1)}, u32[]{:S(2)}, u32[]{:S(2)}) collective-permute-start(bf16[4,16384]{1,0:T(4,128)(2,1)S(1)} %broadcast_select_fusion.4), channel_id=1, source_target_pairs={{0,8},{2,10},{4,12},{6,14},{8,0},{10,2},{12,4},{14,6},{16,24},{18,... | collective-permute-start | bytes 393224 | tf_op jit(solution)/shard_map/ppermute | solution.py:16
  383.7 13.0 %collective-permute-start.2 = (bf16[4,16384]{1,0:T(4,128)(2,1)S(1)}, bf16[4,16384]{1,0:T(4,128)(2,1)S(1)}, u32[]{:S(2)}, u32[]{:S(2)}) collective-permute-start(bf16[4,16384]{1,0:T(4,128)(2,1)S(1)} %broadcast_select_fusion.15), channel_id=1, source_target_pairs={{0,8},{2,10},{4,12},{6,14},{8,0},{10,2},{12,4},{14,6},{16,24},{18,... | collective-permute-start | bytes 393224 | tf_op jit(solution)/shard_map/ppermute | solution.py:16
  386.6 12.3 %collective-permute-start.8 = (bf16[4,16384]{1,0:T(4,128)(2,1)S(1)}, bf16[4,16384]{1,0:T(4,128)(2,1)S(1)}, u32[]{:S(2)}, u32[]{:S(2)}) collective-permute-start(bf16[4,16384]{1,0:T(4,128)(2,1)S(1)} %broadcast_select_fusion.5), channel_id=1, source_target_pairs={{0,8},{2,10},{4,12},{6,14},{8,0},{10,2},{12,4},{14,6},{16,24},{18,... | collective-permute-start | bytes 393224 | tf_op jit(solution)/shard_map/ppermute | solution.py:16
  391.2 7.9 %collective-permute-start.15 = (bf16[4,16384]{1,0:T(4,128)(2,1)S(1)}, bf16[4,16384]{1,0:T(4,128)(2,1)S(1)}, u32[]{:S(2)}, u32[]{:S(2)}) collective-permute-start(bf16[4,16384]{1,0:T(4,128)(2,1)S(1)} %broadcast_select_fusion.16), channel_id=1, source_target_pairs={{0,16},{2,18},{4,20},{6,22},{8,24},{10,26},{12,28},{14,30},{16,0},... | collective-permute-start | bytes 393224 | tf_op jit(solution)/shard_map/ppermute | solution.py:16
  394.0 7.4 %collective-permute-start.21 = (bf16[4,16384]{1,0:T(4,128)(2,1)S(1)}, bf16[4,16384]{1,0:T(4,128)(2,1)S(1)}, u32[]{:S(2)}, u32[]{:S(2)}) collective-permute-start(bf16[4,16384]{1,0:T(4,128)(2,1)S(1)} %broadcast_select_fusion.6), channel_id=1, source_target_pairs={{0,16},{2,18},{4,20},{6,22},{8,24},{10,26},{12,28},{14,30},{16,0},... | collective-permute-start | bytes 393224 | tf_op jit(solution)/shard_map/ppermute | solution.py:16
  396.8 6.2 %collective-permute-start.3 = (bf16[4,16384]{1,0:T(4,128)(2,1)S(1)}, bf16[4,16384]{1,0:T(4,128)(2,1)S(1)}, u32[]{:S(2)}, u32[]{:S(2)}) collective-permute-start(bf16[4,16384]{1,0:T(4,128)(2,1)S(1)} %broadcast_select_fusion.17), channel_id=1, source_target_pairs={{0,16},{2,18},{4,20},{6,22},{8,24},{10,26},{12,28},{14,30},{16,0},... | collective-permute-start | bytes 393224 | tf_op jit(solution)/shard_map/ppermute | solution.py:16
  398.9 6.6 %collective-permute-start.9 = (bf16[4,16384]{1,0:T(4,128)(2,1)S(1)}, bf16[4,16384]{1,0:T(4,128)(2,1)S(1)}, u32[]{:S(2)}, u32[]{:S(2)}) collective-permute-start(bf16[4,16384]{1,0:T(4,128)(2,1)S(1)} %broadcast_select_fusion.7), channel_id=1, source_target_pairs={{0,16},{2,18},{4,20},{6,22},{8,24},{10,26},{12,28},{14,30},{16,0},... | collective-permute-start | bytes 393224 | tf_op jit(solution)/shard_map/ppermute | solution.py:16
  399.2 9.4 %collective-permute-start.16 = (bf16[4,16384]{1,0:T(4,128)(2,1)S(1)}, bf16[4,16384]{1,0:T(4,128)(2,1)S(1)}, u32[]{:S(2)}, u32[]{:S(2)}) collective-permute-start(bf16[4,16384]{1,0:T(4,128)(2,1)S(1)} %broadcast_select_fusion.18), channel_id=1, source_target_pairs={{0,32},{2,34},{4,36},{6,38},{8,40},{10,42},{12,44},{14,46},{16,48}... | collective-permute-start | bytes 393224 | tf_op jit(solution)/shard_map/ppermute | solution.py:16
  401.4 9.9 %collective-permute-start.22 = (bf16[4,16384]{1,0:T(4,128)(2,1)S(1)}, bf16[4,16384]{1,0:T(4,128)(2,1)S(1)}, u32[]{:S(2)}, u32[]{:S(2)}) collective-permute-start(bf16[4,16384]{1,0:T(4,128)(2,1)S(1)} %broadcast_select_fusion.8), channel_id=1, source_target_pairs={{0,32},{2,34},{4,36},{6,38},{8,40},{10,42},{12,44},{14,46},{16,48}... | collective-permute-start | bytes 393224 | tf_op jit(solution)/shard_map/ppermute | solution.py:16
  403.0 11.2 %collective-permute-start.4 = (bf16[4,16384]{1,0:T(4,128)(2,1)S(1)}, bf16[4,16384]{1,0:T(4,128)(2,1)S(1)}, u32[]{:S(2)}, u32[]{:S(2)}) collective-permute-start(bf16[4,16384]{1,0:T(4,128)(2,1)S(1)} %broadcast_select_fusion.19), channel_id=1, source_target_pairs={{0,32},{2,34},{4,36},{6,38},{8,40},{10,42},{12,44},{14,46},{16,48}... | collective-permute-start | bytes 393224 | tf_op jit(solution)/shard_map/ppermute | solution.py:16
  405.6 10.5 %collective-permute-start.10 = (bf16[4,16384]{1,0:T(4,128)(2,1)S(1)}, bf16[4,16384]{1,0:T(4,128)(2,1)S(1)}, u32[]{:S(2)}, u32[]{:S(2)}) collective-permute-start(bf16[4,16384]{1,0:T(4,128)(2,1)S(1)} %broadcast_select_fusion.9), channel_id=1, source_target_pairs={{0,32},{2,34},{4,36},{6,38},{8,40},{10,42},{12,44},{14,46},{16,48}... | collective-permute-start | bytes 393224 | tf_op jit(solution)/shard_map/ppermute | solution.py:16
  408.6 9.4 %collective-permute-start.17 = (bf16[4,16384]{1,0:T(4,128)(2,1)S(1)}, bf16[4,16384]{1,0:T(4,128)(2,1)S(1)}, u32[]{:S(2)}, u32[]{:S(2)}) collective-permute-start(bf16[4,16384]{1,0:T(4,128)(2,1)S(1)} %broadcast_select_fusion.20), channel_id=1, source_target_pairs={{0,64},{2,66},{4,68},{6,70},{8,72},{10,74},{12,76},{14,78},{16,80}... | collective-permute-start | bytes 393224 | tf_op jit(solution)/shard_map/ppermute | solution.py:16
  411.4 7.8 %collective-permute-start.23 = (bf16[4,16384]{1,0:T(4,128)(2,1)S(1)}, bf16[4,16384]{1,0:T(4,128)(2,1)S(1)}, u32[]{:S(2)}, u32[]{:S(2)}) collective-permute-start(bf16[4,16384]{1,0:T(4,128)(2,1)S(1)} %broadcast_select_fusion.10), channel_id=1, source_target_pairs={{0,64},{2,66},{4,68},{6,70},{8,72},{10,74},{12,76},{14,78},{16,80}... | collective-permute-start | bytes 393224 | tf_op jit(solution)/shard_map/ppermute | solution.py:16
  414.2 10.3 %collective-permute-start.5 = (bf16[4,16384]{1,0:T(4,128)(2,1)S(1)}, bf16[4,16384]{1,0:T(4,128)(2,1)S(1)}, u32[]{:S(2)}, u32[]{:S(2)}) collective-permute-start(bf16[4,16384]{1,0:T(4,128)(2,1)S(1)} %broadcast_select_fusion.21), channel_id=1, source_target_pairs={{0,64},{2,66},{4,68},{6,70},{8,72},{10,74},{12,76},{14,78},{16,80}... | collective-permute-start | bytes 393224 | tf_op jit(solution)/shard_map/ppermute | solution.py:16
  416.2 8.4 %collective-permute-start.11 = (bf16[4,16384]{1,0:T(4,128)(2,1)S(1)}, bf16[4,16384]{1,0:T(4,128)(2,1)S(1)}, u32[]{:S(2)}, u32[]{:S(2)}) collective-permute-start(bf16[4,16384]{1,0:T(4,128)(2,1)S(1)} %broadcast_select_fusion.11), channel_id=1, source_target_pairs={{0,64},{2,66},{4,68},{6,70},{8,72},{10,74},{12,76},{14,78},{16,80}... | collective-permute-start | bytes 393224 | tf_op jit(solution)/shard_map/ppermute | solution.py:16
  421.2 7.8 %all-to-all-start.4 = ((bf16[2,128,256]{2,1,0:T(8,128)(2,1)}), bf16[2,128,256]{2,1,0:T(8,128)(2,1)S(1)}, u32[]{:S(2)}, u32[]{:S(2)}) async-start(bf16[2,128,256]{2,1,0:T(8,128)(2,1)} %convert_element_type.74), calls=%async_computation.4 | async-start | bytes 262144 | tf_op jit(solution)/shard_map/all_to_all | solution.py:168
  429.0 7.8 %all-to-all-start.3 = ((bf16[2,128,256]{2,1,0:T(8,128)(2,1)}), bf16[2,128,256]{2,1,0:T(8,128)(2,1)S(1)}, u32[]{:S(2)}, u32[]{:S(2)}) async-start(bf16[2,128,256]{2,1,0:T(8,128)(2,1)} %convert_element_type.70), calls=%async_computation.3 | async-start | bytes 262144 | tf_op jit(solution)/shard_map/all_to_all | solution.py:167
  (42 other events, 123.5 us)
Sparse Core Ops, SparseCore 0:
  16.0 172.3 all-gather.1
